TPU v7x, 512 devices: a whole 4x8x8 slice. The times are simulated.
512 devices in a mesh: row: 32 (over z_hi, y, core), col: 16 (over z_lo, x).
Axes of the slice: x: 4, y: 8, z: 8 (z_hi: 2, z_lo: 4; z = z_hi * 4 + z_lo), core: 2. Of those that a mesh axis runs over, the one named last changes fastest.
Arguments:
- mask_logits: float32 [4096, 2048], P('row', 'col'), may hold values from -6 to 6
- target: float32 [4096, 2048], P('row', 'col'), may hold values from 0 to 1
- weight: float32 [4096, 2048], P('row', 'col'), may hold values from 0.004 to 10, as said below
- kernels: float32 [2, 12288], P(None, ('row', 'col')), may hold values from -3 to 3
Outputs:
- new_logits: float32 [4096, 2048], P('row', 'col')
- loss_value: float32 [], replicated
Inputs may be any that keep to these rules, and one draw needn't show every extreme that they name: `weight`: positive loss weights.
All inputs are finite; a program needn't handle non-finite values.
Results may differ from a plain program's by a relative error of at most 0.0003.
Values sent between devices are 32-bit elements; how exact they have to be, the bound alone decides.
A program may use at most 64 MiB of HBM per device.

v0:
```python
import math
import jax
import jax.numpy as jnp
from jax import lax
from jax.sharding import PartitionSpec as P

HALO = 64
KERNELS = 6
BAND = 32
CONDITIONS = 2
SHARPNESS = 6.0
THRESHOLD = 0.75
STEP = 0.5
EPSILON = 1e-06
DOSES = (1.0, 1.15)


def padded_2(block, sides, width):
    for axis, dim in sides:
        count = lax.axis_size(axis)
        forward = [(i, i + 1) for i in range(count - 1)]
        backward = [(target, source) for source, target in forward]
        low = lax.ppermute(
            lax.slice_in_dim(block, block.shape[dim] - width, None, axis=dim), axis, forward
        )
        high = lax.ppermute(lax.slice_in_dim(block, 0, width, axis=dim), axis, backward)
        block = jnp.concatenate([low, block, high], axis=dim)
    return block


def matmul(first, second):
    return jnp.matmul(
        first, second, precision=lax.Precision.HIGHEST, preferred_element_type=jnp.float32
    )


def cmatmul(first_re, first_im, second_re, second_im):
    return (
        matmul(first_re, second_re) - matmul(first_im, second_im),
        matmul(first_re, second_im) + matmul(first_im, second_re),
    )


def dft_rows(band, pad_width):
    freq = jnp.arange(band, dtype=jnp.int32) - band // 2
    place = jnp.arange(pad_width, dtype=jnp.int32)
    turns = (freq[:, None] * place[None, :] % pad_width).astype(jnp.float32) * (
        2.0 * math.pi / pad_width
    )
    factor = 1.0 / math.sqrt(pad_width)
    return (jnp.cos(turns) * factor, -jnp.sin(turns) * factor)


def synthesize(spec_re, spec_im, wave_re, wave_im):
    left_re, left_im = cmatmul(wave_re.T, -wave_im.T, spec_re, spec_im)
    return cmatmul(left_re, left_im, wave_re, -wave_im)


def analyse(cell_re, cell_im, wave_re, wave_im):
    left_re, left_im = cmatmul(wave_re, wave_im, cell_re, cell_im)
    return cmatmul(left_re, left_im, wave_re.T, wave_im.T)


def tile_terms(padded_tile, kernel_re, kernel_im, wave_re, wave_im, dose, margin):
    mask_tile, target_tile, weight_tile = (padded_tile[0], padded_tile[1], padded_tile[2])
    pad_width = mask_tile.shape[0]
    core_width = pad_width - 2 * margin
    four_re, four_im = cmatmul(
        matmul(wave_re, mask_tile), matmul(wave_im, mask_tile), wave_re.T, wave_im.T
    )
    prod_re = four_re[None] * kernel_re - four_im[None] * kernel_im
    prod_im = four_re[None] * kernel_im + four_im[None] * kernel_re
    fields_re, fields_im = synthesize(prod_re, prod_im, wave_re, wave_im)
    intensity = jnp.sum(fields_re * fields_re + fields_im * fields_im, axis=0)
    resist = jax.nn.sigmoid(SHARPNESS * (dose * intensity - THRESHOLD))
    error_map = resist - target_tile
    inner = (weight_tile * error_map * error_map)[
        margin : margin + core_width, margin : margin + core_width
    ]
    tile_loss = jnp.sum(inner)
    slope_map = 2.0 * SHARPNESS * dose * weight_tile * error_map * resist * (1.0 - resist)
    back_re, back_im = analyse(
        slope_map[None] * fields_re, slope_map[None] * fields_im, wave_re, wave_im
    )
    sum_re = jnp.sum(kernel_re * back_re + kernel_im * back_im, axis=0)
    sum_im = jnp.sum(kernel_re * back_im - kernel_im * back_re, axis=0)
    core_re = wave_re[:, margin : margin + core_width]
    core_im = wave_im[:, margin : margin + core_width]
    left_re, left_im = cmatmul(core_re.T, -core_im.T, sum_re, sum_im)
    real_part = matmul(left_re, core_re) + matmul(left_im, core_im)
    return (2.0 * real_part, tile_loss)


def shards(mask_logits, target, weight, kernels):
    mask_cells = jax.nn.sigmoid(mask_logits)
    stacked = jnp.stack([mask_cells, target, weight])
    padded = padded_2(stacked, (("row", 1), ("col", 2)), HALO)
    core_width = mask_logits.shape[0]
    tile_count = mask_logits.shape[1] // core_width
    pad_width = core_width + 2 * HALO
    wave_re, wave_im = dft_rows(BAND, pad_width)
    whole_bank = lax.all_gather(kernels, ("row", "col"), axis=1, tiled=True)
    tile_grads = [jnp.zeros((core_width, core_width), jnp.float32)]
    loss_global = jnp.float32(0.0)
    for condition in range(CONDITIONS):
        flat_bank = whole_bank[condition]
        spectra = flat_bank.reshape(2, KERNELS, BAND, BAND)
        condition_loss = jnp.float32(0.0)
        part_grad, part_loss = tile_terms(
            padded, spectra[0], spectra[1], wave_re, wave_im, DOSES[condition], HALO
        )
        tile_grads[0] = tile_grads[0] + part_grad
        condition_loss = part_loss
        loss_global = loss_global + lax.psum(condition_loss, ("row", "col"))
    grad_cells = tile_grads[0] * mask_cells * (1.0 - mask_cells)
    square_local = jnp.sum(grad_cells * grad_cells)
    square_global = lax.psum(square_local, ("row", "col"))
    cell_count = lax.axis_size("row") * core_width * lax.axis_size("col") * core_width * tile_count
    loss_value = loss_global / cell_count
    norm_value = jnp.sqrt(square_global / cell_count + EPSILON)
    return (mask_logits - STEP * grad_cells / norm_value, loss_value)


def solution(mesh):
    placed = (P("row", "col"), P("row", "col"), P("row", "col"), P(None, ("row", "col")))
    return jax.shard_map(
        shards, mesh=mesh, in_specs=placed, out_specs=(P("row", "col"), P()), check_vma=False
    )
```

profile of v0, /device:TPU:25, one launch (start us, length us, event | category | flops | bytes accessed | tf_op | source)
XLA Modules:
  0.0 1498.3 jit_solution(4228233007003579788)
XLA Ops:
  0.6 0.9 fusion.144
  1.5 0.9 pad_maximum_fusion.2
  2.4 2.7 collective-permute-start.1
  5.2 4.3 collective-permute-start
  9.5 1274.6 %all-gather = f32[512,24,2]{1,2,0:T(2,128)S(1)} all-gather(f32[1,24,2]{1,2,0:T(2,128)} %bitcast.232), channel_id=1, replica_groups=mesh['row'=32,'col'=16] {'row','col'}, dimensions={0}, use_global_device_ids=true | all-gather | bytes 98496 | tf_op jit(solution)/shard_map/all_gather | solution.py:102
  1285.4 1.3 collective-permute-start.3
  1286.7 4.3 collective-permute-start.2
  1291.0 0.8 negate_multiply_fusion
  1291.8 2.2 collective-permute-done.3
  1294.0 1.5 collective-permute-done.2
  1298.7 0.7 multiply_add_fusion
  1299.5 0.5 fusion.136
  1300.6 0.5 fusion.141
  1301.1 0.5 fusion.134
  1301.6 1.6 fusion.70
  1303.2 2.5 fusion.68
  1305.7 1.6 copy.29
  1307.3 2.1 fusion.132
  1309.4 2.1 fusion.139
  1311.5 1.6 copy.28
  1313.1 1.4 fusion.138
  1314.5 1.4 fusion.130
  1315.9 2.5 fusion.64
  1318.4 1.6 fusion.62
  1320.0 1.8 convolution_subtract_fusion.1
  1321.9 1.7 add_reduce_fusion.1
  1323.6 1.6 convolution_subtract_fusion
  1325.2 1.7 add_reduce_fusion
  1327.1 1.2 fusion.10
  1328.3 1.2 fusion.8
  1329.6 1.3 fusion.19
  1330.9 0.5 fusion.97
  1331.4 0.5 fusion.115
  1331.9 1.2 fusion.2
  1333.1 1.5 fusion
  1334.6 1.3 fusion.31
  1335.9 0.5 fusion.92
  1336.4 0.5 fusion.108
  1337.1 1.2 fusion.25
  1338.4 0.5 convolution_add_fusion.3
  1338.9 0.5 subtract_reduce_fusion.1
  1340.7 1.2 fusion.37
  1342.0 0.5 convolution_add_fusion.2
  1342.5 0.5 subtract_reduce_fusion
  1344.6 0.7 fusion.81
  1346.6 0.9 multiply_reduce_fusion
  1347.6 147.6 %all-reduce = (f32[]{:T(128)}, f32[]{:T(128)}) all-reduce(f32[]{:T(128)} %get-tuple-element.34, f32[]{:T(128)S(6)} %add.285), channel_id=1, replica_groups=mesh['row'=32,'col'=16] {'row','col'}, use_global_device_ids=true, to_apply=%region_7.8 | all-reduce | flops 2 | bytes 16 | tf_op jit(solution)/shard_map/psum | solution.py:117
  1496.5 0.6 divide_subtract_fusion
  (72 shorter events, 8.1 us)
Async XLA Ops:
  2.4 1282.7 %copy-start.13 = (f32[128,128]{1,0:T(8,128)S(1)}, f32[128,128]{1,0:T(8,128)}, u32[]{:S(2)}) copy-start(f32[128,128]{1,0:T(8,128)} %param.6) | copy-start | bytes 196612
  2.4 1282.7 %copy-start.14 = (f32[128,128]{1,0:T(8,128)S(1)}, f32[128,128]{1,0:T(8,128)}, u32[]{:S(2)}) copy-start(f32[128,128]{1,0:T(8,128)} %param.5) | copy-start | bytes 196612
  2.4 1282.7 %collective-permute-start.1 = (f32[3,64,128]{2,1,0:T(8,128)S(1)}, f32[3,64,128]{2,1,0:T(8,128)S(1)}, u32[]{:S(2)}, u32[]{:S(2)}) collective-permute-start(f32[3,64,128]{2,1,0:T(8,128)S(1)} %get-tuple-element.25), channel_id=1, source_target_pairs={{16,0},{32,16},{48,32},{64,48},{80,64},{96,80},{112,96},{128,112},... | collective-permute-start | bytes 294920 | tf_op jit(solution)/shard_map/ppermute | solution.py:26
  5.2 1279.9 %collective-permute-start = (f32[3,64,128]{2,1,0:T(8,128)S(1)}, f32[3,64,128]{2,1,0:T(8,128)S(1)}, u32[]{:S(2)}, u32[]{:S(2)}) collective-permute-start(f32[3,64,128]{2,1,0:T(8,128)S(1)} %get-tuple-element.24), channel_id=1, source_target_pairs={{0,16},{16,32},{32,48},{48,64},{64,80},{80,96},{96,112},{112,128},... | collective-permute-start | bytes 294920 | tf_op jit(solution)/shard_map/ppermute | solution.py:23
  1284.8 13.8 copy-start.9
  1284.9 13.7 copy-start.11
  1285.0 13.7 copy-start.5
  1285.1 13.6 copy-start.7
  1285.4 8.6 collective-permute-start.3
  1286.7 8.8 collective-permute-start.2
  1295.9 0.9 copy-start
  1300.0 1.6 copy-start.4
  1313.1 5.4 copy-start.3
  1321.8 1.7 copy-start.2
  1325.1 1.7 copy-start.1
  1337.1 1.8 copy-start.10
  1337.1 1.8 copy-start.12
  1337.1 2.3 copy-start.17
  1337.1 2.8 copy-start.15
  1339.4 3.1 copy-start.6
  1339.4 3.1 copy-start.8
  1340.7 5.9 copy-start.16
where the time goes:
time: 1500 us
  blocking collectives  1420 us (95%)
  matrix products  44.1 us (3%)
    all_gather x1, blocking collectives, shards(): whole_bank = lax.all_gather(kernels, ('row', 'col'), axis=1, tiled=True)  1270 us
    psum x1, blocking collectives, shards(): square_global = lax.psum(square_local, ('row', 'col'))  148 us
    dot_general x42, matrix products, matmul(): jnp.matmul(first, second, precision=lax.Precision.HIGHEST, preferred_elem...  35.1 us
  transfers between devices with their start and end apart: 4, of which 2 were waited for; matrix products, arithmetic and copies ran while one was open for 0% of the time, Pallas kernels for 0%

commit v1 on v0

--- a/solution.py
+++ b/solution.py
@@ -13,6 +13,13 @@
 STEP = 0.5
 EPSILON = 1e-06
 DOSES = (1.0, 1.15)
+
+
+def exchange_gather(value, name, d):
+    count = lax.axis_size(name)
+    blocks = jnp.stack([value for _ in range(count)])
+    blocks = lax.all_to_all(blocks, name, split_axis=0, concat_axis=0)
+    return jnp.concatenate(blocks, axis=d)
 
 
 def padded_2(block, sides, width):
@@ -99,7 +106,7 @@
     tile_count = mask_logits.shape[1] // core_width
     pad_width = core_width + 2 * HALO
     wave_re, wave_im = dft_rows(BAND, pad_width)
-    whole_bank = lax.all_gather(kernels, ("row", "col"), axis=1, tiled=True)
+    whole_bank = exchange_gather(kernels, ("row", "col"), 1)
     tile_grads = [jnp.zeros((core_width, core_width), jnp.float32)]
     loss_global = jnp.float32(0.0)
     for condition in range(CONDITIONS):

time: 1500 us -> 215 us (0.14)
  the two profiles are of different devices: /device:TPU:25 before, /device:TPU:1 now
where the time goes in v1:
time: 215 us; the launch traced here: 212 us
  blocking collectives  107 us (50%)
  matrix products  44 us (20%)
  starting transfers between devices  36 us (17%)
  waiting for transfers between devices  7.96 us (4%)
  local copies, waits for them, and re-layouts  7.71 us (4%)
  between operations  5.42 us (3%)
  other arithmetic  3.75 us (2%)
    psum x1, blocking collectives, shards(): square_global = lax.psum(square_local, ('row', 'col'))  107 us
    dot_general x42, matrix products, matmul(): jnp.matmul(first, second, precision=lax.Precision.HIGHEST, preferred_elem...  35 us
    all_to_all x1, starting transfers between devices, exchange_gather(): blocks = lax.all_to_all(blocks, name, split_axis=0, concat_axis=0)  22.1 us
    unnamed x8, matrix products  8.98 us
    ppermute x2, starting transfers between devices, padded_2(): lax.ppermute(lax.slice_in_dim(block, 0, width, axis=dim), axis, backward)  7.5 us
    ppermute x2, starting transfers between devices, padded_2(): lax.ppermute(lax.slice_in_dim(block, block.shape[dim] - width, None, axis...  6.4 us
    all_to_all x1, waiting for transfers between devices, exchange_gather(): blocks = lax.all_to_all(blocks, name, split_axis=0, concat_axis=0)  4.57 us
  transfers between devices with their start and end apart: 5, of which 3 were waited for; matrix products, arithmetic and copies ran while one was open for 1% of the time, Pallas kernels for 0%

profile of v1, /device:TPU:1, one launch (start us, length us, event | category | flops | bytes accessed | tf_op | source)
XLA Modules:
  0.0 211.5 jit_solution(749131677239985216)
XLA Ops:
  0.7 1.6 stack.10
  2.3 22.1 %all-to-all-start = ((f32[512,2,24]{2,1,0:T(2,128)}), f32[512,2,24]{2,1,0:T(2,128)S(1)}, u32[]{:S(2)}, u32[]{:S(2)}) async-start(f32[512,2,24]{2,1,0:T(2,128)} %stack.10), calls=%async_computation | async-start | bytes 1048576 | tf_op jit(solution)/shard_map/all_to_all | solution.py:21
  24.6 6.2 %collective-permute-start.1 = (f32[3,64,128]{2,1,0:T(8,128)S(1)}, f32[3,64,128]{2,1,0:T(8,128)S(1)}, u32[]{:S(2)}, u32[]{:S(2)}) collective-permute-start(f32[3,64,128]{2,1,0:T(8,128)S(1)} %get-tuple-element.25), channel_id=1, source_target_pairs={{16,0},{32,16},{48,32},{64,48},{80,64},{96,80},{112,96},{128,112},... | collective-permute-start | bytes 294920 | tf_op jit(solution)/shard_map/ppermute | solution.py:33
  30.8 1.9 collective-permute-start
  32.7 3.0 %collective-permute-done.1 = f32[3,64,128]{2,1,0:T(8,128)S(1)} collective-permute-done((f32[3,64,128]{2,1,0:T(8,128)S(1)}, f32[3,64,128]{2,1,0:T(8,128)S(1)}, u32[]{:S(2)}, u32[]{:S(2)}) %collective-permute-start.1) | collective-permute-done | bytes 98336 | tf_op jit(solution)/shard_map/ppermute | solution.py:33
  36.0 1.3 collective-permute-start.3
  37.3 4.5 %collective-permute-start.2 = (f32[3,256,64]{2,1,0:T(8,128)S(1)}, f32[3,256,64]{2,1,0:T(8,128)S(1)}, u32[]{:S(2)}, u32[]{:S(2)}) collective-permute-start(f32[3,256,64]{2,1,0:T(8,128)S(1)} %get-tuple-element.18), channel_id=1, source_target_pairs={{0,1},{1,2},{2,3},{3,4},{4,5},{5,6},{6,7},{7,8},{8,9},{9,10},{10,1... | collective-permute-start | bytes 589832 | tf_op jit(solution)/shard_map/ppermute | solution.py:30
  41.7 0.8 negate_multiply_fusion
  42.6 4.6 %all-to-all-done = f32[512,2,24]{2,1,0:T(2,128)S(1)} async-done(((f32[512,2,24]{2,1,0:T(2,128)}), f32[512,2,24]{2,1,0:T(2,128)S(1)}, u32[]{:S(2)}, u32[]{:S(2)}) %all-to-all-start) | async-done | bytes 98336 | tf_op jit(solution)/shard_map/all_to_all | solution.py:21
  47.2 1.5 slice_reduce_fusion.1
  52.7 0.7 multiply_add_fusion
  53.5 0.5 fusion.136
  54.6 0.5 fusion.141
  55.1 0.5 fusion.134
  55.7 1.6 fusion.70
  57.2 2.5 %fusion.68 = f32[6,256,256]{2,1,0:T(8,128)S(1)} fusion(f32[256,6,32]{0,2,1:T(8,128)S(1)} %bitcast.210, f32[256,6,32]{0,2,1:T(8,128)} %bitcast.208, s32[32]{0:T(128)S(1)} %iota_add_fusion), kind=kOutput, calls=%fused_computation.84 | convolution fusion | flops 151183360 | bytes 1966208 | tf_op jit(solution)/shard_map/dot_general | solution.py:39
  59.7 1.6 copy.27
  61.4 2.1 fusion.132
  63.4 2.1 fusion.139
  65.5 1.6 copy.26
  67.1 1.4 fusion.138
  68.6 1.4 fusion.130
  70.0 2.7 %fusion.64 = f32[6,256,256]{2,1,0:T(8,128)S(1)} fusion(f32[256,6,32]{0,2,1:T(8,128)S(1)} %bitcast.211, f32[256,6,32]{0,2,1:T(8,128)} %bitcast.205, s32[32]{0:T(128)S(1)} %iota_add_fusion), kind=kOutput, calls=%fused_computation.80 | convolution fusion | flops 151166976 | bytes 1966208 | tf_op jit(solution)/shard_map/dot_general | solution.py:39
  72.7 1.6 fusion.62
  74.2 1.6 convolution_subtract_fusion.1
  75.8 1.7 add_reduce_fusion.1
  77.5 1.6 convolution_subtract_fusion
  79.1 1.7 add_reduce_fusion
  81.1 1.2 fusion.10
  82.3 1.2 fusion.8
  83.6 1.3 fusion.19
  84.8 0.5 fusion.97
  85.3 0.7 fusion.115
  86.1 1.2 fusion.2
  87.3 1.2 fusion
  88.6 1.3 fusion.31
  89.8 0.5 fusion.92
  90.3 0.5 fusion.108
  91.1 1.2 fusion.25
  92.3 0.5 convolution_add_fusion.3
  92.8 0.5 subtract_reduce_fusion.1
  94.7 1.2 fusion.37
  95.9 0.5 convolution_add_fusion.2
  96.4 0.5 subtract_reduce_fusion
  98.5 0.7 fusion.81
  100.6 0.9 multiply_reduce_fusion
  101.5 106.7 %all-reduce = (f32[]{:T(128)}, f32[]{:T(128)}) all-reduce(f32[]{:T(128)} %get-tuple-element.34, f32[]{:T(128)S(6)} %add.285), channel_id=1, replica_groups=mesh['row'=32,'col'=16] {'row','col'}, use_global_device_ids=true, to_apply=%region_7.8 | all-reduce | flops 2 | bytes 16 | tf_op jit(solution)/shard_map/psum | solution.py:124
  209.5 0.6 divide_subtract_fusion
  (74 shorter events, 8.0 us)
Async XLA Ops:
  0.6 23.8 %copy-start.16 = (f32[128,128]{1,0:T(8,128)S(1)}, f32[128,128]{1,0:T(8,128)}, u32[]{:S(2)}) copy-start(f32[128,128]{1,0:T(8,128)} %param.4) | copy-start | bytes 196612
  0.6 23.9 %copy-start.13 = (f32[128,128]{1,0:T(8,128)S(1)}, f32[128,128]{1,0:T(8,128)}, u32[]{:S(2)}) copy-start(f32[128,128]{1,0:T(8,128)} %param.6) | copy-start | bytes 196612
  0.7 23.9 %copy-start.14 = (f32[128,128]{1,0:T(8,128)S(1)}, f32[128,128]{1,0:T(8,128)}, u32[]{:S(2)}) copy-start(f32[128,128]{1,0:T(8,128)} %param.5) | copy-start | bytes 196612
  2.3 44.8 %all-to-all-start = ((f32[512,2,24]{2,1,0:T(2,128)}), f32[512,2,24]{2,1,0:T(2,128)S(1)}, u32[]{:S(2)}, u32[]{:S(2)}) async-start(f32[512,2,24]{2,1,0:T(2,128)} %stack.10), calls=%async_computation | async-start | bytes 1048576 | tf_op jit(solution)/shard_map/all_to_all | solution.py:21
  24.6 11.2 %collective-permute-start.1 = (f32[3,64,128]{2,1,0:T(8,128)S(1)}, f32[3,64,128]{2,1,0:T(8,128)S(1)}, u32[]{:S(2)}, u32[]{:S(2)}) collective-permute-start(f32[3,64,128]{2,1,0:T(8,128)S(1)} %get-tuple-element.25), channel_id=1, source_target_pairs={{16,0},{32,16},{48,32},{64,48},{80,64},{96,80},{112,96},{128,112},... | collective-permute-start | bytes 294920 | tf_op jit(solution)/shard_map/ppermute | solution.py:33
  30.8 5.0 %collective-permute-start = (f32[3,64,128]{2,1,0:T(8,128)S(1)}, f32[3,64,128]{2,1,0:T(8,128)S(1)}, u32[]{:S(2)}, u32[]{:S(2)}) collective-permute-start(f32[3,64,128]{2,1,0:T(8,128)S(1)} %get-tuple-element.24), channel_id=1, source_target_pairs={{0,16},{16,32},{32,48},{48,64},{64,80},{80,96},{96,112},{112,128},... | collective-permute-start | bytes 294920 | tf_op jit(solution)/shard_map/ppermute | solution.py:30
  36.0 13.2 %collective-permute-start.3 = (f32[3,256,64]{2,1,0:T(8,128)S(1)}, f32[3,256,64]{2,1,0:T(8,128)S(1)}, u32[]{:S(2)}, u32[]{:S(2)}) collective-permute-start(f32[3,256,64]{2,1,0:T(8,128)S(1)} %get-tuple-element.19), channel_id=1, source_target_pairs={{1,0},{2,1},{3,2},{4,3},{5,4},{6,5},{7,6},{8,7},{9,8},{10,9},{11,1... | collective-permute-start | bytes 589832 | tf_op jit(solution)/shard_map/ppermute | solution.py:33
  37.3 12.2 %collective-permute-start.2 = (f32[3,256,64]{2,1,0:T(8,128)S(1)}, f32[3,256,64]{2,1,0:T(8,128)S(1)}, u32[]{:S(2)}, u32[]{:S(2)}) collective-permute-start(f32[3,256,64]{2,1,0:T(8,128)S(1)} %get-tuple-element.18), channel_id=1, source_target_pairs={{0,1},{1,2},{2,3},{3,4},{4,5},{5,6},{6,7},{7,8},{8,9},{9,10},{10,1... | collective-permute-start | bytes 589832 | tf_op jit(solution)/shard_map/ppermute | solution.py:30
  48.7 3.9 %copy-start.9 = (f32[6,32,32]{2,1,0:T(8,128)}, f32[6,32,32]{2,1,0:T(8,128)S(1)}, u32[]{:S(2)}) copy-start(f32[6,32,32]{2,1,0:T(8,128)S(1)} %squeeze.26) | copy-start | bytes 73732
  48.9 3.8 %copy-start.11 = (f32[6,32,32]{2,1,0:T(8,128)}, f32[6,32,32]{2,1,0:T(8,128)S(1)}, u32[]{:S(2)}) copy-start(f32[6,32,32]{2,1,0:T(8,128)S(1)} %squeeze.24) | copy-start | bytes 73732
  49.0 3.7 %copy-start.5 = (f32[6,32,32]{2,1,0:T(8,128)}, f32[6,32,32]{2,1,0:T(8,128)S(1)}, u32[]{:S(2)}) copy-start(f32[6,32,32]{2,1,0:T(8,128)S(1)} %squeeze.27) | copy-start | bytes 73732
  49.1 3.6 %copy-start.7 = (f32[6,32,32]{2,1,0:T(8,128)}, f32[6,32,32]{2,1,0:T(8,128)S(1)}, u32[]{:S(2)}) copy-start(f32[6,32,32]{2,1,0:T(8,128)S(1)} %squeeze.28) | copy-start | bytes 73732
  49.9 0.9 copy-start
  54.0 1.6 copy-start.4
  67.1 5.5 %copy-start.3 = (f32[256,192]{0,1:S(1)}, f32[256,192]{0,1}, u32[]{:S(2)}) copy-start(f32[256,192]{0,1} %fusion.132) | copy-start | bytes 589828
  75.8 1.7 copy-start.2
  79.1 1.7 copy-start.1
  91.0 1.8 copy-start.10
  91.0 1.8 copy-start.12
  91.0 2.3 %copy-start.18 = (f32[32,256]{1,0:T(8,128)S(1)}, f32[32,256]{1,0:T(8,128)}, u32[]{:S(2)}) copy-start(f32[32,256]{1,0:T(8,128)} %get-tuple-element.29) | copy-start | bytes 98308
  91.0 2.8 %copy-start.15 = (f32[32,256]{1,0:T(8,128)S(1)}, f32[32,256]{1,0:T(8,128)}, u32[]{:S(2)}) copy-start(f32[32,256]{1,0:T(8,128)} %get-tuple-element.28) | copy-start | bytes 98308
  93.3 3.1 %copy-start.6 = (f32[6,32,32]{2,1,0:T(8,128)S(1)}, f32[6,32,32]{2,1,0:T(8,128)}, u32[]{:S(2)}) copy-start(f32[6,32,32]{2,1,0:T(8,128)} %copy-done.5) | copy-start | bytes 73732
  93.4 3.1 %copy-start.8 = (f32[6,32,32]{2,1,0:T(8,128)S(1)}, f32[6,32,32]{2,1,0:T(8,128)}, u32[]{:S(2)}) copy-start(f32[6,32,32]{2,1,0:T(8,128)} %copy-done.7) | copy-start | bytes 73732
  94.6 5.9 %copy-start.17 = (f32[128,128]{1,0:T(8,128)S(1)}, f32[128,128]{1,0:T(8,128)}, u32[]{:S(2)}) copy-start(f32[128,128]{1,0:T(8,128)} %param.4) | copy-start | bytes 196612
